TPU v7x, 128 devices: a whole 4x4x4 slice. The times are simulated.
128 devices in a mesh: grp: 16 (over x, y_lo, core), blk: 8 (over z, y_hi).
Axes of the slice: x: 4, y: 4 (y_hi: 2, y_lo: 2; y = y_hi * 2 + y_lo), z: 4, core: 2. Of those that a mesh axis runs over, the one named last changes fastest.
Arguments:
- nodes: float32 [16, 3, 128, 256], P('grp', None, 'blk'), may hold values from -4 to 4
- panels: float32 [16, 3, 4096], P('grp', None, 'blk'), may hold values from -4 to 4
- nu_field: float32 [16, 128, 256], P('grp', 'blk'), may hold values from 0.2 to 1.5
- vorticity: float32 [16, 128, 256], P('grp', 'blk'), may hold values from 1 to 100
- flow: float32 [16, 4, 128, 256], P('grp', None, 'blk'), may hold values from -6 to 6
- fringe_block: int32 [16384], P(('grp', 'blk')), may hold values from 0 to 31
- fringe_size: int32 [16384], P(('grp', 'blk')), may hold values from 1 to 128
- fringe_owner: int32 [16384, 1], P(('grp', 'blk')), may hold values from 0 to 127; in each aligned block of 128 rows (0 to 127, 128 to 255, ...) at most 2 rows name the same one
- fringe_cell: int32 [16384], P(('grp', 'blk')), may hold values from 0 to 15
Outputs:
- wall_distance: float32 [16, 128, 256], P('grp', 'blk')
- nu_next: float32 [16, 128, 256], P('grp', 'blk')
- offbody: float32 [2048, 5, 128], P(('grp', 'blk'))
Inputs may be any that keep to these rules, and one draw needn't show every extreme that they name: `fringe_owner`: among the 128 slots of one device, at most 2 name the same owner device.
All inputs are finite; a program needn't handle non-finite values.
Results may differ from a plain program's by a relative error of at most 0.00012.
Values sent between devices are 32-bit elements; how exact they have to be, the bound alone decides.
No kernel may reach another device: no remote copies, remote signals or barrier semaphores. Data moves between devices by JAX's collectives and lax.ppermute only.
A program may use at most 64 MiB of HBM per device.

v0:
```python
import math
import jax
import jax.numpy as jnp
from jax import lax
from jax.sharding import PartitionSpec as P

BLOCK = 128
VARS = 5
CAP = 2
OB = 16


def padded_2(cells, sides, width):
    for axis, dim in sides:
        count = lax.axis_size(axis)
        head = lax.slice_in_dim(cells, 0, width, axis=dim)
        tail = lax.slice_in_dim(cells, cells.shape[dim] - width, cells.shape[dim], axis=dim)
        cells = jnp.concatenate(
            [
                lax.ppermute(tail, axis, [(i, (i + 1) % count) for i in range(count)]),
                cells,
                lax.ppermute(head, axis, [((i + 1) % count, i) for i in range(count)]),
            ],
            axis=dim,
        )
    return cells


def sa_step(nu_ext, dist, vort):
    centre = nu_ext[1:-1]
    east = nu_ext[2:]
    west = nu_ext[:-2]
    padded = jnp.pad(centre, ((0, 0), (1, 1)))
    north = padded[:, 2:]
    south = padded[:, :-2]
    flux = (1.0 + 0.5 * (centre + east)) * (east - centre) - (1.0 + 0.5 * (centre + west)) * (
        centre - west
    )
    flux = (
        flux
        + (1.0 + 0.5 * (centre + north)) * (north - centre)
        - (1.0 + 0.5 * (centre + south)) * (centre - south)
    )
    grads = 0.25 * ((east - west) * (east - west) + (north - south) * (north - south))
    diffusion = (flux + 0.622 * grads) / (2.0 / 3.0)
    ratio = centre / dist
    return centre + 0.02 * (0.1355 * vort * centre - 3.24 * ratio * ratio + diffusion)


def per_device(
    nodes, panels, nu_field, vorticity, flow, fringe_block, fringe_size, fringe_owner, fringe_cell
):
    lines = nodes.shape[2]
    points_j = nodes.shape[3]
    points = nodes[0].reshape(3, -1)
    init = jnp.full((points.shape[1],), 1e30, jnp.float32)
    piece = lax.all_gather(panels[0], "blk", axis=1, tiled=True)
    count = piece.shape[1]
    width = math.gcd(count, 256)
    blocks = jnp.transpose(piece.reshape(3, count // width, width), (1, 0, 2))

    def visit(carry, panel_block):
        delta0 = points[0][:, None] - panel_block[0][None, :]
        delta1 = points[1][:, None] - panel_block[1][None, :]
        delta2 = points[2][:, None] - panel_block[2][None, :]
        dsq = delta0 * delta0 + delta1 * delta1 + delta2 * delta2
        return (jnp.minimum(carry, jnp.min(dsq, axis=1)), None)

    result, unused = lax.scan(visit, init, blocks)
    dist = jnp.sqrt(result + 0.25).reshape(lines, points_j)
    vort = vorticity[0]
    nu_now = nu_field[0]
    for step in range(2):
        ext = padded_2(nu_now, (("blk", 0),), 1)
        nu_now = sa_step(ext, dist, vort)
    state = jnp.concatenate([nu_now[None], flow[0]], axis=0)
    state = state.reshape(VARS, lines * (points_j // BLOCK), BLOCK)
    values = jnp.transpose(jnp.take(state, fringe_block, axis=1), (1, 0, 2))
    live = (jnp.arange(BLOCK, dtype=jnp.int32)[None, :] < fringe_size[:, None]).astype(jnp.float32)
    values = values * live[:, None, :]
    group_count = lax.axis_size("grp")
    member_count = lax.axis_size("blk")
    devices_all = group_count * member_count
    dest = fringe_owner[:, 0]
    hits = (dest[:, None] == jnp.arange(devices_all, dtype=jnp.int32)[None, :]).astype(jnp.int32)
    rank = jnp.sum((jnp.cumsum(hits, axis=0) - hits) * hits, axis=1)
    slot = dest * CAP + rank
    buffer = jnp.zeros((devices_all * CAP, VARS, BLOCK), jnp.float32).at[slot].set(values)
    cells = (
        jnp.zeros((devices_all * CAP,), jnp.float32).at[slot].set(fringe_cell.astype(jnp.float32))
    )
    got_values, got_cells = (
        lax.all_to_all(
            buffer.reshape(devices_all, CAP, VARS, BLOCK),
            ("grp", "blk"),
            split_axis=0,
            concat_axis=0,
            tiled=True,
        ),
        lax.all_to_all(
            cells.reshape(devices_all, CAP), ("grp", "blk"), split_axis=0, concat_axis=0, tiled=True
        ),
    )
    rows = got_values.reshape(devices_all * CAP, VARS * BLOCK)
    flat_cells = got_cells.reshape(devices_all * CAP)
    select = (flat_cells[None, :] == jnp.arange(OB, dtype=jnp.float32)[:, None]).astype(jnp.float32)
    offbody = jnp.dot(
        select, rows, precision=lax.Precision.HIGHEST, preferred_element_type=jnp.float32
    )
    return (dist[None], nu_now[None], offbody.reshape(OB, VARS, BLOCK))


def solution(mesh):
    in_specs = (
        P("grp", None, "blk", None),
        P("grp", None, "blk"),
        P("grp", "blk", None),
        P("grp", "blk", None),
        P("grp", None, "blk", None),
        P(("grp", "blk")),
        P(("grp", "blk")),
        P(("grp", "blk"), None),
        P(("grp", "blk")),
    )
    out_specs = (P("grp", "blk", None), P("grp", "blk", None), P(("grp", "blk"), None, None))
    return jax.shard_map(
        per_device, mesh=mesh, in_specs=in_specs, out_specs=out_specs, check_vma=False
    )
```

profile of v0, /device:TPU:1, one launch (start us, length us, event | category | flops | bytes accessed | tf_op | source)
XLA Modules:
  0.0 139.1 jit_solution(15647237432715452222)
XLA Ops:
  0.6 0.7 slice_bitcast_fusion.1
  1.4 7.2 %collective-permute-start = (f32[1,256]{1,0:T(1,128)S(1)}, f32[1,256]{1,0:T(1,128)S(1)}, u32[]{:S(2)}, u32[]{:S(2)}) collective-permute-start(f32[1,256]{1,0:T(1,128)S(1)} %get-tuple-element.73), channel_id=1, source_target_pairs={{1,0},{2,1},{3,2},{4,3},{5,4},{6,5},{7,6},{0,7},{9,8},{10,9},{11,1... | collective-permute-start | bytes 3080 | tf_op jit(solution)/shard_map/ppermute | solution.py:22
  8.6 0.7 fusion
  9.3 0.2 reduce_window_sum.11
  9.5 0.8 select_reduce_fusion
  10.3 0.7 fusion.52
  11.0 0.7 convert_element_type.18
  11.6 1.0 scatter_custom_fusion
  12.6 0.8 all_to_all.9
  13.4 9.9 %all-to-all-start = ((f32[128,1,2]{2,1,0:T(1,128)}), f32[128,1,2]{2,1,0:T(1,128)S(1)}, u32[]{:S(2)}, u32[]{:S(2)}) async-start(f32[128,1,2]{2,1,0:T(1,128)} %bitcast.9), calls=%async_computation | async-start | bytes 131072 | tf_op jit(solution)/shard_map/all_to_all | solution.py:100
  23.3 26.8 %all-gather = f32[1,3,4096]{2,0,1:T(1,128)S(1)} all-gather(f32[1,3,512]{2,0,1:T(1,128)} %param.12), channel_id=2, replica_groups=mesh['grp'=16,'blk'=8] {'blk'}, dimensions={2}, use_global_device_ids=true | all-gather | bytes 55296 | tf_op jit(solution)/shard_map/all_gather | solution.py:57
  50.2 0.1 reduce
  50.3 0.8 copy.41
  51.1 43.5 %while.11 = (s32[]{:T(128)}, f32[4096]{0:T(1024)S(1)}, f32[3,4096]{1,0:T(4,128)S(1)}, f32[16,3,256]{2,0,1:T(8,128)S(1)}, s32[]{:T(128)}, /*index=5*/s32[]{:T(128)}, s32[]{}, s32[]{}) while((s32[]{:T(128)}, f32[4096]{0:T(1024)S(1)}, f32[3,4096]{1,0:T(4,128)S(1)}, f32[16,3,256]{2,0,1:T(8,128)S(1)}, s32[]{:T(128)}, ...), condition=%wide.region_2.3_spmd.clone, body=%wide.region_0.2_spmd.clone.sunk | while | flops 9441285 | bytes 222339 | solution.py:69
  51.2 2.6 %add_reduce_fusion.2 = f32[4096]{0:T(1024)S(1)} fusion(f32[256]{0:T(256)S(1)} %bitcast.82, f32[4096]{0:T(1024)S(1)} %bitcast.76, f32[256]{0:T(256)S(1)} %bitcast.81, f32[4096]{0:T(1024)S(1)} %bitcast.77, f32[256]{0:T(256)S(1)} %bitcast.80, f32[4096]{0:T(1024)S(1)} %bitcast.75), kind=kLoop, calls=%fused_computation.3.clone.1 | loop fusion | flops 9433088 | bytes 68608 | tf_op jit(solution)/shard_map/while/body/eval_jaxpr/reduce_min | solution.py:67
  53.9 2.6 %add_reduce_fusion.2 = f32[4096]{0:T(1024)S(1)} fusion(f32[256]{0:T(256)S(1)} %bitcast.82, f32[4096]{0:T(1024)S(1)} %bitcast.76, f32[256]{0:T(256)S(1)} %bitcast.81, f32[4096]{0:T(1024)S(1)} %bitcast.77, f32[256]{0:T(256)S(1)} %bitcast.80, f32[4096]{0:T(1024)S(1)} %bitcast.75), kind=kLoop, calls=%fused_computation.3.clone.1 | loop fusion | flops 9433088 | bytes 68608 | tf_op jit(solution)/shard_map/while/body/eval_jaxpr/reduce_min | solution.py:67
  56.7 2.6 %add_reduce_fusion.2 = f32[4096]{0:T(1024)S(1)} fusion(f32[256]{0:T(256)S(1)} %bitcast.82, f32[4096]{0:T(1024)S(1)} %bitcast.76, f32[256]{0:T(256)S(1)} %bitcast.81, f32[4096]{0:T(1024)S(1)} %bitcast.77, f32[256]{0:T(256)S(1)} %bitcast.80, f32[4096]{0:T(1024)S(1)} %bitcast.75), kind=kLoop, calls=%fused_computation.3.clone.1 | loop fusion | flops 9433088 | bytes 68608 | tf_op jit(solution)/shard_map/while/body/eval_jaxpr/reduce_min | solution.py:67
  59.4 2.6 %add_reduce_fusion.2 = f32[4096]{0:T(1024)S(1)} fusion(f32[256]{0:T(256)S(1)} %bitcast.82, f32[4096]{0:T(1024)S(1)} %bitcast.76, f32[256]{0:T(256)S(1)} %bitcast.81, f32[4096]{0:T(1024)S(1)} %bitcast.77, f32[256]{0:T(256)S(1)} %bitcast.80, f32[4096]{0:T(1024)S(1)} %bitcast.75), kind=kLoop, calls=%fused_computation.3.clone.1 | loop fusion | flops 9433088 | bytes 68608 | tf_op jit(solution)/shard_map/while/body/eval_jaxpr/reduce_min | solution.py:67
  62.1 2.6 %add_reduce_fusion.2 = f32[4096]{0:T(1024)S(1)} fusion(f32[256]{0:T(256)S(1)} %bitcast.82, f32[4096]{0:T(1024)S(1)} %bitcast.76, f32[256]{0:T(256)S(1)} %bitcast.81, f32[4096]{0:T(1024)S(1)} %bitcast.77, f32[256]{0:T(256)S(1)} %bitcast.80, f32[4096]{0:T(1024)S(1)} %bitcast.75), kind=kLoop, calls=%fused_computation.3.clone.1 | loop fusion | flops 9433088 | bytes 68608 | tf_op jit(solution)/shard_map/while/body/eval_jaxpr/reduce_min | solution.py:67
  64.8 2.6 %add_reduce_fusion.2 = f32[4096]{0:T(1024)S(1)} fusion(f32[256]{0:T(256)S(1)} %bitcast.82, f32[4096]{0:T(1024)S(1)} %bitcast.76, f32[256]{0:T(256)S(1)} %bitcast.81, f32[4096]{0:T(1024)S(1)} %bitcast.77, f32[256]{0:T(256)S(1)} %bitcast.80, f32[4096]{0:T(1024)S(1)} %bitcast.75), kind=kLoop, calls=%fused_computation.3.clone.1 | loop fusion | flops 9433088 | bytes 68608 | tf_op jit(solution)/shard_map/while/body/eval_jaxpr/reduce_min | solution.py:67
  67.5 2.6 %add_reduce_fusion.2 = f32[4096]{0:T(1024)S(1)} fusion(f32[256]{0:T(256)S(1)} %bitcast.82, f32[4096]{0:T(1024)S(1)} %bitcast.76, f32[256]{0:T(256)S(1)} %bitcast.81, f32[4096]{0:T(1024)S(1)} %bitcast.77, f32[256]{0:T(256)S(1)} %bitcast.80, f32[4096]{0:T(1024)S(1)} %bitcast.75), kind=kLoop, calls=%fused_computation.3.clone.1 | loop fusion | flops 9433088 | bytes 68608 | tf_op jit(solution)/shard_map/while/body/eval_jaxpr/reduce_min | solution.py:67
  70.3 2.6 %add_reduce_fusion.2 = f32[4096]{0:T(1024)S(1)} fusion(f32[256]{0:T(256)S(1)} %bitcast.82, f32[4096]{0:T(1024)S(1)} %bitcast.76, f32[256]{0:T(256)S(1)} %bitcast.81, f32[4096]{0:T(1024)S(1)} %bitcast.77, f32[256]{0:T(256)S(1)} %bitcast.80, f32[4096]{0:T(1024)S(1)} %bitcast.75), kind=kLoop, calls=%fused_computation.3.clone.1 | loop fusion | flops 9433088 | bytes 68608 | tf_op jit(solution)/shard_map/while/body/eval_jaxpr/reduce_min | solution.py:67
  73.0 2.6 %add_reduce_fusion.2 = f32[4096]{0:T(1024)S(1)} fusion(f32[256]{0:T(256)S(1)} %bitcast.82, f32[4096]{0:T(1024)S(1)} %bitcast.76, f32[256]{0:T(256)S(1)} %bitcast.81, f32[4096]{0:T(1024)S(1)} %bitcast.77, f32[256]{0:T(256)S(1)} %bitcast.80, f32[4096]{0:T(1024)S(1)} %bitcast.75), kind=kLoop, calls=%fused_computation.3.clone.1 | loop fusion | flops 9433088 | bytes 68608 | tf_op jit(solution)/shard_map/while/body/eval_jaxpr/reduce_min | solution.py:67
  75.7 2.6 %add_reduce_fusion.2 = f32[4096]{0:T(1024)S(1)} fusion(f32[256]{0:T(256)S(1)} %bitcast.82, f32[4096]{0:T(1024)S(1)} %bitcast.76, f32[256]{0:T(256)S(1)} %bitcast.81, f32[4096]{0:T(1024)S(1)} %bitcast.77, f32[256]{0:T(256)S(1)} %bitcast.80, f32[4096]{0:T(1024)S(1)} %bitcast.75), kind=kLoop, calls=%fused_computation.3.clone.1 | loop fusion | flops 9433088 | bytes 68608 | tf_op jit(solution)/shard_map/while/body/eval_jaxpr/reduce_min | solution.py:67
  78.4 2.6 %add_reduce_fusion.2 = f32[4096]{0:T(1024)S(1)} fusion(f32[256]{0:T(256)S(1)} %bitcast.82, f32[4096]{0:T(1024)S(1)} %bitcast.76, f32[256]{0:T(256)S(1)} %bitcast.81, f32[4096]{0:T(1024)S(1)} %bitcast.77, f32[256]{0:T(256)S(1)} %bitcast.80, f32[4096]{0:T(1024)S(1)} %bitcast.75), kind=kLoop, calls=%fused_computation.3.clone.1 | loop fusion | flops 9433088 | bytes 68608 | tf_op jit(solution)/shard_map/while/body/eval_jaxpr/reduce_min | solution.py:67
  81.1 2.6 %add_reduce_fusion.2 = f32[4096]{0:T(1024)S(1)} fusion(f32[256]{0:T(256)S(1)} %bitcast.82, f32[4096]{0:T(1024)S(1)} %bitcast.76, f32[256]{0:T(256)S(1)} %bitcast.81, f32[4096]{0:T(1024)S(1)} %bitcast.77, f32[256]{0:T(256)S(1)} %bitcast.80, f32[4096]{0:T(1024)S(1)} %bitcast.75), kind=kLoop, calls=%fused_computation.3.clone.1 | loop fusion | flops 9433088 | bytes 68608 | tf_op jit(solution)/shard_map/while/body/eval_jaxpr/reduce_min | solution.py:67
  83.9 2.6 %add_reduce_fusion.2 = f32[4096]{0:T(1024)S(1)} fusion(f32[256]{0:T(256)S(1)} %bitcast.82, f32[4096]{0:T(1024)S(1)} %bitcast.76, f32[256]{0:T(256)S(1)} %bitcast.81, f32[4096]{0:T(1024)S(1)} %bitcast.77, f32[256]{0:T(256)S(1)} %bitcast.80, f32[4096]{0:T(1024)S(1)} %bitcast.75), kind=kLoop, calls=%fused_computation.3.clone.1 | loop fusion | flops 9433088 | bytes 68608 | tf_op jit(solution)/shard_map/while/body/eval_jaxpr/reduce_min | solution.py:67
  86.6 2.6 %add_reduce_fusion.2 = f32[4096]{0:T(1024)S(1)} fusion(f32[256]{0:T(256)S(1)} %bitcast.82, f32[4096]{0:T(1024)S(1)} %bitcast.76, f32[256]{0:T(256)S(1)} %bitcast.81, f32[4096]{0:T(1024)S(1)} %bitcast.77, f32[256]{0:T(256)S(1)} %bitcast.80, f32[4096]{0:T(1024)S(1)} %bitcast.75), kind=kLoop, calls=%fused_computation.3.clone.1 | loop fusion | flops 9433088 | bytes 68608 | tf_op jit(solution)/shard_map/while/body/eval_jaxpr/reduce_min | solution.py:67
  89.3 2.6 %add_reduce_fusion.2 = f32[4096]{0:T(1024)S(1)} fusion(f32[256]{0:T(256)S(1)} %bitcast.82, f32[4096]{0:T(1024)S(1)} %bitcast.76, f32[256]{0:T(256)S(1)} %bitcast.81, f32[4096]{0:T(1024)S(1)} %bitcast.77, f32[256]{0:T(256)S(1)} %bitcast.80, f32[4096]{0:T(1024)S(1)} %bitcast.75), kind=kLoop, calls=%fused_computation.3.clone.1 | loop fusion | flops 9433088 | bytes 68608 | tf_op jit(solution)/shard_map/while/body/eval_jaxpr/reduce_min | solution.py:67
  92.0 2.6 %add_reduce_fusion.2 = f32[4096]{0:T(1024)S(1)} fusion(f32[256]{0:T(256)S(1)} %bitcast.82, f32[4096]{0:T(1024)S(1)} %bitcast.76, f32[256]{0:T(256)S(1)} %bitcast.81, f32[4096]{0:T(1024)S(1)} %bitcast.77, f32[256]{0:T(256)S(1)} %bitcast.80, f32[4096]{0:T(1024)S(1)} %bitcast.75), kind=kLoop, calls=%fused_computation.3.clone.1 | loop fusion | flops 9433088 | bytes 68608 | tf_op jit(solution)/shard_map/while/body/eval_jaxpr/reduce_min | solution.py:67
  94.9 0.1 fusion.5
  95.0 3.5 %collective-permute-start.2 = (f32[1,256]{1,0:T(1,128)S(1)}, f32[1,256]{1,0:T(1,128)S(1)}, u32[]{:S(2)}, u32[]{:S(2)}) collective-permute-start(f32[1,256]{1,0:T(1,128)S(1)} %get-tuple-element.71), channel_id=1, source_target_pairs={{1,0},{2,1},{3,2},{4,3},{5,4},{6,5},{7,6},{0,7},{9,8},{10,9},{11,1... | collective-permute-start | bytes 3080 | tf_op jit(solution)/shard_map/ppermute | solution.py:22
  98.6 0.6 collective-permute-done.2
  99.2 5.3 %collective-permute-done.3 = f32[1,256]{1,0:T(1,128)S(1)} collective-permute-done((f32[1,256]{1,0:T(1,128)S(1)}, f32[1,256]{1,0:T(1,128)S(1)}, u32[]{:S(2)}, u32[]{:S(2)}) %collective-permute-start.3) | collective-permute-done | bytes 1056 | tf_op jit(solution)/shard_map/ppermute | solution.py:20
  104.7 0.8 gather_fusion
  105.5 0.2 select_multiply_fusion
  105.8 4.3 %scatter_fusion = f32[256,5,128]{2,1,0:T(8,128)S(1)} fusion(f32[256,5,128]{2,1,0:T(8,128)S(1)} %broadcast_in_dim.35, s32[128]{0:T(128)S(1)} %fusion.52, f32[128,5,128]{2,1,0:T(8,128)S(1)} %select_multiply_fusion), kind=kCustom, calls=%fused_computation.2 | custom fusion | bytes 983552 | tf_op jit(solution)/shard_map/scatter | solution.py:88
  110.1 1.2 copy.32
  111.3 10.9 %all-to-all-start.1 = ((f32[128,2,5,128]{3,1,2,0:T(2,128)}), f32[128,2,5,128]{3,1,2,0:T(2,128)S(1)}, u32[]{:S(2)}, u32[]{:S(2)}) async-start(f32[128,2,5,128]{3,1,2,0:T(2,128)} %copy.32), calls=%async_computation.1 | async-start | bytes 1310720 | tf_op jit(solution)/shard_map/all_to_all | solution.py:93
  122.2 0.6 broadcast_in_dim_reshape.4
  122.8 0.5 broadcast.112
  123.3 0.8 reduce.4
  124.1 0.1 eq.36
  124.3 13.3 %all-to-all-done.1 = f32[128,2,5,128]{3,1,2,0:T(2,128)S(1)} async-done(((f32[128,2,5,128]{3,1,2,0:T(2,128)}), f32[128,2,5,128]{3,1,2,0:T(2,128)S(1)}, u32[]{:S(2)}, u32[]{:S(2)}) %all-to-all-start.1) | async-done | bytes 655392 | tf_op jit(solution)/shard_map/all_to_all | solution.py:93
  137.6 0.1 copy.33
  137.7 0.1 copy.46
  137.8 0.2 copy.34
  138.1 1.0 fusion.49
  (80 shorter events, 1.4 us)
Async XLA Ops:
  1.4 93.5 %collective-permute-start = (f32[1,256]{1,0:T(1,128)S(1)}, f32[1,256]{1,0:T(1,128)S(1)}, u32[]{:S(2)}, u32[]{:S(2)}) collective-permute-start(f32[1,256]{1,0:T(1,128)S(1)} %get-tuple-element.73), channel_id=1, source_target_pairs={{1,0},{2,1},{3,2},{4,3},{5,4},{6,5},{7,6},{0,7},{9,8},{10,9},{11,1... | collective-permute-start | bytes 3080 | tf_op jit(solution)/shard_map/ppermute | solution.py:22
  8.6 86.3 %collective-permute-start.1 = (f32[1,256]{1,0:T(1,128)S(1)}, f32[1,256]{1,0:T(1,128)S(1)}, u32[]{:S(2)}, u32[]{:S(2)}) collective-permute-start(f32[1,256]{1,0:T(1,128)S(1)} %get-tuple-element.74), channel_id=1, source_target_pairs={{0,1},{1,2},{2,3},{3,4},{4,5},{5,6},{6,7},{7,0},{8,9},{9,10},{10,1... | collective-permute-start | bytes 3080 | tf_op jit(solution)/shard_map/ppermute | solution.py:20
  12.6 82.1 %copy-start.5 = (s32[128]{0:T(128)S(1)}, s32[128]{0:T(128)}, u32[]{:S(2)}) copy-start(s32[128]{0:T(128)} %param.16) | copy-start | bytes 1540
  12.6 82.1 %copy-start.4 = (s32[128]{0:T(128)S(1)}, s32[128]{0:T(128)}, u32[]{:S(2)}) copy-start(s32[128]{0:T(128)} %param.17) | copy-start | bytes 1540
  13.4 81.5 %copy-start.2 = (f32[1,16,256]{2,1,0:T(8,128)S(1)}, f32[1,16,256]{2,1,0:T(8,128)}, u32[]{:S(2)}) copy-start(f32[1,16,256]{2,1,0:T(8,128)} %param.14) | copy-start | bytes 49156
  13.4 81.5 %copy-start.3 = (f32[1,16,256]{2,1,0:T(8,128)S(1)}, f32[1,16,256]{2,1,0:T(8,128)}, u32[]{:S(2)}) copy-start(f32[1,16,256]{2,1,0:T(8,128)} %param.13) | copy-start | bytes 49156
  13.4 97.9 %all-to-all-start = ((f32[128,1,2]{2,1,0:T(1,128)}), f32[128,1,2]{2,1,0:T(1,128)S(1)}, u32[]{:S(2)}, u32[]{:S(2)}) async-start(f32[128,1,2]{2,1,0:T(1,128)} %bitcast.9), calls=%async_computation | async-start | bytes 131072 | tf_op jit(solution)/shard_map/all_to_all | solution.py:100
  23.3 75.2 %copy-start = (f32[1,4,16,256]{3,2,1,0:T(8,128)S(1)}, f32[1,4,16,256]{3,2,1,0:T(8,128)}, u32[]{:S(2)}) copy-start(f32[1,4,16,256]{3,2,1,0:T(8,128)} %param.15) | copy-start | bytes 196612
  95.0 4.3 %collective-permute-start.2 = (f32[1,256]{1,0:T(1,128)S(1)}, f32[1,256]{1,0:T(1,128)S(1)}, u32[]{:S(2)}, u32[]{:S(2)}) collective-permute-start(f32[1,256]{1,0:T(1,128)S(1)} %get-tuple-element.71), channel_id=1, source_target_pairs={{1,0},{2,1},{3,2},{4,3},{5,4},{6,5},{7,6},{0,7},{9,8},{10,9},{11,1... | collective-permute-start | bytes 3080 | tf_op jit(solution)/shard_map/ppermute | solution.py:22
  98.5 6.0 %collective-permute-start.3 = (f32[1,256]{1,0:T(1,128)S(1)}, f32[1,256]{1,0:T(1,128)S(1)}, u32[]{:S(2)}, u32[]{:S(2)}) collective-permute-start(f32[1,256]{1,0:T(1,128)S(1)} %get-tuple-element.72), channel_id=1, source_target_pairs={{0,1},{1,2},{2,3},{3,4},{4,5},{5,6},{6,7},{7,0},{8,9},{9,10},{10,1... | collective-permute-start | bytes 3080 | tf_op jit(solution)/shard_map/ppermute | solution.py:20
  104.6 1.1 copy-start.1
  111.3 26.3 %all-to-all-start.1 = ((f32[128,2,5,128]{3,1,2,0:T(2,128)}), f32[128,2,5,128]{3,1,2,0:T(2,128)S(1)}, u32[]{:S(2)}, u32[]{:S(2)}) async-start(f32[128,2,5,128]{3,1,2,0:T(2,128)} %copy.32), calls=%async_computation.1 | async-start | bytes 1310720 | tf_op jit(solution)/shard_map/all_to_all | solution.py:93
where the time goes:
time: 140 us; the launch traced here: 139 us
  other arithmetic  46.4 us (33%)
  starting transfers between devices  31.6 us (23%)
  blocking collectives  26.8 us (19%)
  waiting for transfers between devices  19.3 us (14%)
  local copies, waits for them, and re-layouts  12.3 us (9%)
    reduce_min x16, other arithmetic, visit(): return (jnp.minimum(carry, jnp.min(dsq, axis=1)), None)  41.7 us
    all_gather x1, blocking collectives, per_device(): piece = lax.all_gather(panels[0], 'blk', axis=1, tiled=True)  26.8 us
    all_to_all x1, waiting for transfers between devices, per_device(): lax.all_to_all(buffer.reshape(devices_all, CAP, VARS, BLOCK), ('grp', 'bl...  13.3 us
    all_to_all x1, starting transfers between devices, per_device(): lax.all_to_all(buffer.reshape(devices_all, CAP, VARS, BLOCK), ('grp', 'bl...  10.9 us
    ppermute x2, starting transfers between devices, padded_2(): lax.ppermute(head, axis, [((i + 1) % count, i) for i in range(count)])  10.7 us
    all_to_all x1, starting transfers between devices, per_device(): lax.all_to_all(cells.reshape(devices_all, CAP), ('grp', 'blk'), split_axi...  9.92 us
    ppermute x2, waiting for transfers between devices, padded_2(): lax.ppermute(tail, axis, [(i, (i + 1) % count) for i in range(count)])  5.31 us
    scatter x1, local copies, waits for them, and re-layouts, per_device(): jnp.zeros((devices_all * CAP, VARS, BLOCK), jnp.float32).at[slot]  4.3 us
  transfers between devices with their start and end apart: 6, of which 3 were waited for; matrix products, arithmetic and copies ran while one was open for 41% of the time, Pallas kernels for 0%

commit v1 on v0

--- a/solution.py
+++ b/solution.py
@@ -54,7 +54,9 @@
     points_j = nodes.shape[3]
     points = nodes[0].reshape(3, -1)
     init = jnp.full((points.shape[1],), 1e30, jnp.float32)
-    piece = lax.all_gather(panels[0], "blk", axis=1, tiled=True)
+    piece = jnp.concatenate(
+        lax.all_to_all(jnp.stack([panels[0]] * lax.axis_size("blk")), "blk", 0, 0), axis=1
+    )
     count = piece.shape[1]
     width = math.gcd(count, 256)
     blocks = jnp.transpose(piece.reshape(3, count // width, width), (1, 0, 2))

time: 140 us -> 120 us (0.86)
  blocking collectives: 26.8 us -> 0 us
  starting transfers between devices: 31.6 us -> 35.6 us
  other arithmetic: 46.4 us -> 48.2 us
    all_gather x1 -> x0, blocking collectives: 26.8 us -> none  [per_device(): piece = lax.all_gather(panels[0], 'blk', axis=1, tiled=True)]
    all_to_all x0 -> x1, starting transfers between devices: none -> 8.48 us  [per_device(): lax.all_to_all(jnp.stack([panels[0]] * lax.axis_size('blk')), 'blk', 0, 0)]
    all_to_all x1, starting transfers between devices: 10.9 us -> 5.75 us  [per_device(): lax.all_to_all(buffer.reshape(devices_all, CAP, VARS, BLOCK), ('grp', 'bl...]
  transfers between devices with their start and end apart: 6 -> 7, of which waited for: 3 -> 3; matrix products, arithmetic and copies ran while one was open for 41% -> 50% of each run, Pallas kernels for 0% -> 0%
where the time goes in v1:
time: 120 us; the launch traced here: 119 us
  other arithmetic  48.2 us (40%)
  starting transfers between devices  35.6 us (30%)
  waiting for transfers between devices  19.3 us (16%)
  local copies, waits for them, and re-layouts  13.6 us (11%)
    reduce_min x16, other arithmetic, visit(): return (jnp.minimum(carry, jnp.min(dsq, axis=1)), None)  41.7 us
    all_to_all x1, waiting for transfers between devices, per_device(): lax.all_to_all(buffer.reshape(devices_all, CAP, VARS, BLOCK), ('grp', 'bl...  13.3 us
    ppermute x2, starting transfers between devices, padded_2(): lax.ppermute(head, axis, [((i + 1) % count, i) for i in range(count)])  10.9 us
    all_to_all x1, starting transfers between devices, per_device(): lax.all_to_all(cells.reshape(devices_all, CAP), ('grp', 'blk'), split_axi...  10.5 us
    all_to_all x1, starting transfers between devices, per_device(): lax.all_to_all(jnp.stack([panels[0]] * lax.axis_size('blk')), 'blk', 0, 0)  8.48 us
    all_to_all x1, starting transfers between devices, per_device(): lax.all_to_all(buffer.reshape(devices_all, CAP, VARS, BLOCK), ('grp', 'bl...  5.75 us
    ppermute x2, waiting for transfers between devices, padded_2(): lax.ppermute(tail, axis, [(i, (i + 1) % count) for i in range(count)])  5.31 us
    scatter x1, local copies, waits for them, and re-layouts, per_device(): jnp.zeros((devices_all * CAP, VARS, BLOCK), jnp.float32).at[slot]  4.3 us
  transfers between devices with their start and end apart: 7, of which 3 were waited for; matrix products, arithmetic and copies ran while one was open for 50% of the time, Pallas kernels for 0%

profile of v1, /device:TPU:1, one launch (start us, length us, event | category | flops | bytes accessed | tf_op | source)
XLA Modules:
  0.0 119.4 jit_solution(11892178275012597096)
XLA Ops:
  0.6 0.7 copy.39
  1.3 0.6 stack.3
  2.0 8.5 %all-to-all-start = ((f32[8,3,512]{2,1,0:T(4,128)}), f32[8,3,512]{2,1,0:T(4,128)S(1)}, u32[]{:S(2)}, u32[]{:S(2)}) async-start(f32[8,3,512]{2,1,0:T(4,128)} %stack.3), calls=%async_computation | async-start | bytes 131072 | tf_op jit(solution)/shard_map/all_to_all | solution.py:58
  10.4 0.7 slice_bitcast_fusion.1
  11.2 5.1 %collective-permute-start = (f32[1,256]{1,0:T(1,128)S(1)}, f32[1,256]{1,0:T(1,128)S(1)}, u32[]{:S(2)}, u32[]{:S(2)}) collective-permute-start(f32[1,256]{1,0:T(1,128)S(1)} %get-tuple-element.57), channel_id=1, source_target_pairs={{1,0},{2,1},{3,2},{4,3},{5,4},{6,5},{7,6},{0,7},{9,8},{10,9},{11,1... | collective-permute-start | bytes 3080 | tf_op jit(solution)/shard_map/ppermute | solution.py:22
  16.2 0.7 compare_select_fusion
  16.9 0.7 fusion.1
  17.7 0.7 fusion
  18.4 0.2 reduce_window_sum.11
  18.6 0.8 select_reduce_fusion
  19.4 0.7 fusion.52
  20.1 0.7 compare_and_fusion
  20.8 0.8 copy.34
  21.6 0.7 convert_element_type.18
  22.3 1.0 scatter_custom_fusion
  23.2 0.8 all_to_all.13
  24.0 10.5 %all-to-all-start.1 = ((f32[128,1,2]{2,1,0:T(1,128)}), f32[128,1,2]{2,1,0:T(1,128)S(1)}, u32[]{:S(2)}, u32[]{:S(2)}) async-start(f32[128,1,2]{2,1,0:T(1,128)} %bitcast.11), calls=%async_computation.1 | async-start | bytes 131072 | tf_op jit(solution)/shard_map/all_to_all | solution.py:102
  34.5 43.4 %while.11 = (s32[]{:T(128)}, f32[4096]{0:T(1024)S(1)}, f32[3,4096]{1,0:T(4,128)S(1)}, f32[16,3,256]{2,1,0:T(4,128)S(1)}, s32[]{:T(128)}, /*index=5*/s32[]{:T(128)}, s32[]{}, s32[]{}) while((s32[]{:T(128)}, f32[4096]{0:T(1024)S(1)}, f32[3,4096]{1,0:T(4,128)S(1)}, f32[16,3,256]{2,1,0:T(4,128)S(1)}, s32[]{:T(128)}, ...), condition=%wide.region_2.3_spmd.clone, body=%wide.region_0.2_spmd.clone.sunk | while | flops 9441285 | bytes 222339 | solution.py:71
  34.6 2.6 %add_reduce_fusion.2 = f32[4096]{0:T(1024)S(1)} fusion(f32[256]{0:T(256)S(1)} %bitcast.76, f32[4096]{0:T(1024)S(1)} %bitcast.71, f32[256]{0:T(256)S(1)} %bitcast.75, f32[4096]{0:T(1024)S(1)} %bitcast.72, f32[256]{0:T(256)S(1)} %bitcast.74, f32[4096]{0:T(1024)S(1)} %bitcast.70), kind=kLoop, calls=%fused_computation.3.clone.1 | loop fusion | flops 9433088 | bytes 68608 | tf_op jit(solution)/shard_map/while/body/eval_jaxpr/reduce_min | solution.py:69
  37.3 2.6 %add_reduce_fusion.2 = f32[4096]{0:T(1024)S(1)} fusion(f32[256]{0:T(256)S(1)} %bitcast.76, f32[4096]{0:T(1024)S(1)} %bitcast.71, f32[256]{0:T(256)S(1)} %bitcast.75, f32[4096]{0:T(1024)S(1)} %bitcast.72, f32[256]{0:T(256)S(1)} %bitcast.74, f32[4096]{0:T(1024)S(1)} %bitcast.70), kind=kLoop, calls=%fused_computation.3.clone.1 | loop fusion | flops 9433088 | bytes 68608 | tf_op jit(solution)/shard_map/while/body/eval_jaxpr/reduce_min | solution.py:69
  40.0 2.6 %add_reduce_fusion.2 = f32[4096]{0:T(1024)S(1)} fusion(f32[256]{0:T(256)S(1)} %bitcast.76, f32[4096]{0:T(1024)S(1)} %bitcast.71, f32[256]{0:T(256)S(1)} %bitcast.75, f32[4096]{0:T(1024)S(1)} %bitcast.72, f32[256]{0:T(256)S(1)} %bitcast.74, f32[4096]{0:T(1024)S(1)} %bitcast.70), kind=kLoop, calls=%fused_computation.3.clone.1 | loop fusion | flops 9433088 | bytes 68608 | tf_op jit(solution)/shard_map/while/body/eval_jaxpr/reduce_min | solution.py:69
  42.7 2.6 %add_reduce_fusion.2 = f32[4096]{0:T(1024)S(1)} fusion(f32[256]{0:T(256)S(1)} %bitcast.76, f32[4096]{0:T(1024)S(1)} %bitcast.71, f32[256]{0:T(256)S(1)} %bitcast.75, f32[4096]{0:T(1024)S(1)} %bitcast.72, f32[256]{0:T(256)S(1)} %bitcast.74, f32[4096]{0:T(1024)S(1)} %bitcast.70), kind=kLoop, calls=%fused_computation.3.clone.1 | loop fusion | flops 9433088 | bytes 68608 | tf_op jit(solution)/shard_map/while/body/eval_jaxpr/reduce_min | solution.py:69
  45.4 2.6 %add_reduce_fusion.2 = f32[4096]{0:T(1024)S(1)} fusion(f32[256]{0:T(256)S(1)} %bitcast.76, f32[4096]{0:T(1024)S(1)} %bitcast.71, f32[256]{0:T(256)S(1)} %bitcast.75, f32[4096]{0:T(1024)S(1)} %bitcast.72, f32[256]{0:T(256)S(1)} %bitcast.74, f32[4096]{0:T(1024)S(1)} %bitcast.70), kind=kLoop, calls=%fused_computation.3.clone.1 | loop fusion | flops 9433088 | bytes 68608 | tf_op jit(solution)/shard_map/while/body/eval_jaxpr/reduce_min | solution.py:69
  48.1 2.6 %add_reduce_fusion.2 = f32[4096]{0:T(1024)S(1)} fusion(f32[256]{0:T(256)S(1)} %bitcast.76, f32[4096]{0:T(1024)S(1)} %bitcast.71, f32[256]{0:T(256)S(1)} %bitcast.75, f32[4096]{0:T(1024)S(1)} %bitcast.72, f32[256]{0:T(256)S(1)} %bitcast.74, f32[4096]{0:T(1024)S(1)} %bitcast.70), kind=kLoop, calls=%fused_computation.3.clone.1 | loop fusion | flops 9433088 | bytes 68608 | tf_op jit(solution)/shard_map/while/body/eval_jaxpr/reduce_min | solution.py:69
  50.8 2.6 %add_reduce_fusion.2 = f32[4096]{0:T(1024)S(1)} fusion(f32[256]{0:T(256)S(1)} %bitcast.76, f32[4096]{0:T(1024)S(1)} %bitcast.71, f32[256]{0:T(256)S(1)} %bitcast.75, f32[4096]{0:T(1024)S(1)} %bitcast.72, f32[256]{0:T(256)S(1)} %bitcast.74, f32[4096]{0:T(1024)S(1)} %bitcast.70), kind=kLoop, calls=%fused_computation.3.clone.1 | loop fusion | flops 9433088 | bytes 68608 | tf_op jit(solution)/shard_map/while/body/eval_jaxpr/reduce_min | solution.py:69
  53.6 2.6 %add_reduce_fusion.2 = f32[4096]{0:T(1024)S(1)} fusion(f32[256]{0:T(256)S(1)} %bitcast.76, f32[4096]{0:T(1024)S(1)} %bitcast.71, f32[256]{0:T(256)S(1)} %bitcast.75, f32[4096]{0:T(1024)S(1)} %bitcast.72, f32[256]{0:T(256)S(1)} %bitcast.74, f32[4096]{0:T(1024)S(1)} %bitcast.70), kind=kLoop, calls=%fused_computation.3.clone.1 | loop fusion | flops 9433088 | bytes 68608 | tf_op jit(solution)/shard_map/while/body/eval_jaxpr/reduce_min | solution.py:69
  56.3 2.6 %add_reduce_fusion.2 = f32[4096]{0:T(1024)S(1)} fusion(f32[256]{0:T(256)S(1)} %bitcast.76, f32[4096]{0:T(1024)S(1)} %bitcast.71, f32[256]{0:T(256)S(1)} %bitcast.75, f32[4096]{0:T(1024)S(1)} %bitcast.72, f32[256]{0:T(256)S(1)} %bitcast.74, f32[4096]{0:T(1024)S(1)} %bitcast.70), kind=kLoop, calls=%fused_computation.3.clone.1 | loop fusion | flops 9433088 | bytes 68608 | tf_op jit(solution)/shard_map/while/body/eval_jaxpr/reduce_min | solution.py:69
  59.0 2.6 %add_reduce_fusion.2 = f32[4096]{0:T(1024)S(1)} fusion(f32[256]{0:T(256)S(1)} %bitcast.76, f32[4096]{0:T(1024)S(1)} %bitcast.71, f32[256]{0:T(256)S(1)} %bitcast.75, f32[4096]{0:T(1024)S(1)} %bitcast.72, f32[256]{0:T(256)S(1)} %bitcast.74, f32[4096]{0:T(1024)S(1)} %bitcast.70), kind=kLoop, calls=%fused_computation.3.clone.1 | loop fusion | flops 9433088 | bytes 68608 | tf_op jit(solution)/shard_map/while/body/eval_jaxpr/reduce_min | solution.py:69
  61.7 2.6 %add_reduce_fusion.2 = f32[4096]{0:T(1024)S(1)} fusion(f32[256]{0:T(256)S(1)} %bitcast.76, f32[4096]{0:T(1024)S(1)} %bitcast.71, f32[256]{0:T(256)S(1)} %bitcast.75, f32[4096]{0:T(1024)S(1)} %bitcast.72, f32[256]{0:T(256)S(1)} %bitcast.74, f32[4096]{0:T(1024)S(1)} %bitcast.70), kind=kLoop, calls=%fused_computation.3.clone.1 | loop fusion | flops 9433088 | bytes 68608 | tf_op jit(solution)/shard_map/while/body/eval_jaxpr/reduce_min | solution.py:69
  64.4 2.6 %add_reduce_fusion.2 = f32[4096]{0:T(1024)S(1)} fusion(f32[256]{0:T(256)S(1)} %bitcast.76, f32[4096]{0:T(1024)S(1)} %bitcast.71, f32[256]{0:T(256)S(1)} %bitcast.75, f32[4096]{0:T(1024)S(1)} %bitcast.72, f32[256]{0:T(256)S(1)} %bitcast.74, f32[4096]{0:T(1024)S(1)} %bitcast.70), kind=kLoop, calls=%fused_computation.3.clone.1 | loop fusion | flops 9433088 | bytes 68608 | tf_op jit(solution)/shard_map/while/body/eval_jaxpr/reduce_min | solution.py:69
  67.1 2.6 %add_reduce_fusion.2 = f32[4096]{0:T(1024)S(1)} fusion(f32[256]{0:T(256)S(1)} %bitcast.76, f32[4096]{0:T(1024)S(1)} %bitcast.71, f32[256]{0:T(256)S(1)} %bitcast.75, f32[4096]{0:T(1024)S(1)} %bitcast.72, f32[256]{0:T(256)S(1)} %bitcast.74, f32[4096]{0:T(1024)S(1)} %bitcast.70), kind=kLoop, calls=%fused_computation.3.clone.1 | loop fusion | flops 9433088 | bytes 68608 | tf_op jit(solution)/shard_map/while/body/eval_jaxpr/reduce_min | solution.py:69
  69.8 2.6 %add_reduce_fusion.2 = f32[4096]{0:T(1024)S(1)} fusion(f32[256]{0:T(256)S(1)} %bitcast.76, f32[4096]{0:T(1024)S(1)} %bitcast.71, f32[256]{0:T(256)S(1)} %bitcast.75, f32[4096]{0:T(1024)S(1)} %bitcast.72, f32[256]{0:T(256)S(1)} %bitcast.74, f32[4096]{0:T(1024)S(1)} %bitcast.70), kind=kLoop, calls=%fused_computation.3.clone.1 | loop fusion | flops 9433088 | bytes 68608 | tf_op jit(solution)/shard_map/while/body/eval_jaxpr/reduce_min | solution.py:69
  72.6 2.6 %add_reduce_fusion.2 = f32[4096]{0:T(1024)S(1)} fusion(f32[256]{0:T(256)S(1)} %bitcast.76, f32[4096]{0:T(1024)S(1)} %bitcast.71, f32[256]{0:T(256)S(1)} %bitcast.75, f32[4096]{0:T(1024)S(1)} %bitcast.72, f32[256]{0:T(256)S(1)} %bitcast.74, f32[4096]{0:T(1024)S(1)} %bitcast.70), kind=kLoop, calls=%fused_computation.3.clone.1 | loop fusion | flops 9433088 | bytes 68608 | tf_op jit(solution)/shard_map/while/body/eval_jaxpr/reduce_min | solution.py:69
  75.3 2.6 %add_reduce_fusion.2 = f32[4096]{0:T(1024)S(1)} fusion(f32[256]{0:T(256)S(1)} %bitcast.76, f32[4096]{0:T(1024)S(1)} %bitcast.71, f32[256]{0:T(256)S(1)} %bitcast.75, f32[4096]{0:T(1024)S(1)} %bitcast.72, f32[256]{0:T(256)S(1)} %bitcast.74, f32[4096]{0:T(1024)S(1)} %bitcast.70), kind=kLoop, calls=%fused_computation.3.clone.1 | loop fusion | flops 9433088 | bytes 68608 | tf_op jit(solution)/shard_map/while/body/eval_jaxpr/reduce_min | solution.py:69
  78.1 5.8 %collective-permute-start.2 = (f32[1,256]{1,0:T(1,128)S(1)}, f32[1,256]{1,0:T(1,128)S(1)}, u32[]{:S(2)}, u32[]{:S(2)}) collective-permute-start(f32[1,256]{1,0:T(1,128)S(1)} %get-tuple-element.55), channel_id=1, source_target_pairs={{1,0},{2,1},{3,2},{4,3},{5,4},{6,5},{7,6},{0,7},{9,8},{10,9},{11,1... | collective-permute-start | bytes 3080 | tf_op jit(solution)/shard_map/ppermute | solution.py:22
  84.0 0.6 collective-permute-done.2
  84.7 5.3 %collective-permute-done.3 = f32[1,256]{1,0:T(1,128)S(1)} collective-permute-done((f32[1,256]{1,0:T(1,128)S(1)}, f32[1,256]{1,0:T(1,128)S(1)}, u32[]{:S(2)}, u32[]{:S(2)}) %collective-permute-start.3) | collective-permute-done | bytes 1056 | tf_op jit(solution)/shard_map/ppermute | solution.py:20
  90.2 0.8 gather_fusion
  90.9 0.2 select_multiply_fusion
  91.2 4.3 %scatter_fusion = f32[256,5,128]{2,1,0:T(8,128)S(1)} fusion(f32[256,5,128]{2,1,0:T(8,128)S(1)} %broadcast_in_dim.35, s32[128]{0:T(128)S(1)} %fusion.52, f32[128,5,128]{2,1,0:T(8,128)S(1)} %select_multiply_fusion), kind=kCustom, calls=%fused_computation.2 | custom fusion | bytes 983552 | tf_op jit(solution)/shard_map/scatter | solution.py:90
  95.5 1.2 copy.28
  96.7 5.7 %all-to-all-start.2 = ((f32[128,2,5,128]{3,1,2,0:T(2,128)}), f32[128,2,5,128]{3,1,2,0:T(2,128)S(1)}, u32[]{:S(2)}, u32[]{:S(2)}) async-start(f32[128,2,5,128]{3,1,2,0:T(2,128)} %copy.28), calls=%async_computation.2 | async-start | bytes 1310720 | tf_op jit(solution)/shard_map/all_to_all | solution.py:95
  102.5 0.5 broadcast.112
  103.0 0.8 reduce.3
  103.9 0.6 broadcast_in_dim_reshape.4
  104.5 13.3 %all-to-all-done.2 = f32[128,2,5,128]{3,1,2,0:T(2,128)S(1)} async-done(((f32[128,2,5,128]{3,1,2,0:T(2,128)}), f32[128,2,5,128]{3,1,2,0:T(2,128)S(1)}, u32[]{:S(2)}, u32[]{:S(2)}) %all-to-all-start.2) | async-done | bytes 655392 | tf_op jit(solution)/shard_map/all_to_all | solution.py:95
  118.1 0.2 copy.30
  118.3 1.0 fusion.49
  (77 shorter events, 1.7 us)
Async XLA Ops:
  2.0 22.0 %all-to-all-start = ((f32[8,3,512]{2,1,0:T(4,128)}), f32[8,3,512]{2,1,0:T(4,128)S(1)}, u32[]{:S(2)}, u32[]{:S(2)}) async-start(f32[8,3,512]{2,1,0:T(4,128)} %stack.3), calls=%async_computation | async-start | bytes 131072 | tf_op jit(solution)/shard_map/all_to_all | solution.py:58
  11.2 66.8 %collective-permute-start = (f32[1,256]{1,0:T(1,128)S(1)}, f32[1,256]{1,0:T(1,128)S(1)}, u32[]{:S(2)}, u32[]{:S(2)}) collective-permute-start(f32[1,256]{1,0:T(1,128)S(1)} %get-tuple-element.57), channel_id=1, source_target_pairs={{1,0},{2,1},{3,2},{4,3},{5,4},{6,5},{7,6},{0,7},{9,8},{10,9},{11,1... | collective-permute-start | bytes 3080 | tf_op jit(solution)/shard_map/ppermute | solution.py:22
  16.2 61.7 %collective-permute-start.1 = (f32[1,256]{1,0:T(1,128)S(1)}, f32[1,256]{1,0:T(1,128)S(1)}, u32[]{:S(2)}, u32[]{:S(2)}) collective-permute-start(f32[1,256]{1,0:T(1,128)S(1)} %get-tuple-element.58), channel_id=1, source_target_pairs={{0,1},{1,2},{2,3},{3,4},{4,5},{5,6},{6,7},{7,0},{8,9},{9,10},{10,1... | collective-permute-start | bytes 3080 | tf_op jit(solution)/shard_map/ppermute | solution.py:20
  17.6 60.3 %copy-start.2 = (f32[1,16,256]{2,1,0:T(8,128)S(1)}, f32[1,16,256]{2,1,0:T(8,128)}, u32[]{:S(2)}) copy-start(f32[1,16,256]{2,1,0:T(8,128)} %param.14) | copy-start | bytes 49156
  17.6 60.3 %copy-start.3 = (f32[1,16,256]{2,1,0:T(8,128)S(1)}, f32[1,16,256]{2,1,0:T(8,128)}, u32[]{:S(2)}) copy-start(f32[1,16,256]{2,1,0:T(8,128)} %param.13) | copy-start | bytes 49156
  18.4 65.5 %copy-start = (f32[1,4,16,256]{3,2,1,0:T(8,128)S(1)}, f32[1,4,16,256]{3,2,1,0:T(8,128)}, u32[]{:S(2)}) copy-start(f32[1,4,16,256]{3,2,1,0:T(8,128)} %param.15) | copy-start | bytes 196612
  24.0 72.7 %all-to-all-start.1 = ((f32[128,1,2]{2,1,0:T(1,128)}), f32[128,1,2]{2,1,0:T(1,128)S(1)}, u32[]{:S(2)}, u32[]{:S(2)}) async-start(f32[128,1,2]{2,1,0:T(1,128)} %bitcast.11), calls=%async_computation.1 | async-start | bytes 131072 | tf_op jit(solution)/shard_map/all_to_all | solution.py:102
  78.1 6.6 %collective-permute-start.2 = (f32[1,256]{1,0:T(1,128)S(1)}, f32[1,256]{1,0:T(1,128)S(1)}, u32[]{:S(2)}, u32[]{:S(2)}) collective-permute-start(f32[1,256]{1,0:T(1,128)S(1)} %get-tuple-element.55), channel_id=1, source_target_pairs={{1,0},{2,1},{3,2},{4,3},{5,4},{6,5},{7,6},{0,7},{9,8},{10,9},{11,1... | collective-permute-start | bytes 3080 | tf_op jit(solution)/shard_map/ppermute | solution.py:22
  83.9 6.0 %collective-permute-start.3 = (f32[1,256]{1,0:T(1,128)S(1)}, f32[1,256]{1,0:T(1,128)S(1)}, u32[]{:S(2)}, u32[]{:S(2)}) collective-permute-start(f32[1,256]{1,0:T(1,128)S(1)} %get-tuple-element.56), channel_id=1, source_target_pairs={{0,1},{1,2},{2,3},{3,4},{4,5},{5,6},{6,7},{7,0},{8,9},{9,10},{10,1... | collective-permute-start | bytes 3080 | tf_op jit(solution)/shard_map/ppermute | solution.py:20
  90.1 1.1 copy-start.1
  96.7 21.1 %all-to-all-start.2 = ((f32[128,2,5,128]{3,1,2,0:T(2,128)}), f32[128,2,5,128]{3,1,2,0:T(2,128)S(1)}, u32[]{:S(2)}, u32[]{:S(2)}) async-start(f32[128,2,5,128]{3,1,2,0:T(2,128)} %copy.28), calls=%async_computation.2 | async-start | bytes 1310720 | tf_op jit(solution)/shard_map/all_to_all | solution.py:95
